TPU v7x, 512 devices: a whole 4x4x16 slice. The times are simulated.
512 devices in a mesh: row: 16 (over y, z_hi), col: 32 (over z_lo, x, core).
Axes of the slice: x: 4, y: 4, z: 16 (z_hi: 4, z_lo: 4; z = z_hi * 4 + z_lo), core: 2. Of those that a mesh axis runs over, the one named last changes fastest.
Arguments:
- normals: float32 [12288, 12288], P('row', 'col'), may hold values from -1 to 4, as said below
- design: float32 [512, 12288], P('row', 'col'), may hold values from -0.25 to 0.25
- filter_blocks: float32 [2, 32, 32], replicated, may hold values from -4 to 4, as said below
- regular: float32 [12288], replicated, may hold values from 0.1 to 1
Outputs:
- factored: float32 [12288, 12288], P('row', 'col')
Inputs may be any that keep to these rules, and one draw needn't show every extreme that they name: normals is symmetric; each diagonal entry is at least 1 and each off-diagonal entry has magnitude at most 1 / 256. filter_blocks[0][i, j] = f[i - j] for i >= j and 0 above the diagonal; filter_blocks[1][i, j] = f[32 + i - j] for j >= i and 0 below; f holds the 33 taps of one causal filter with f[0] at least 1.
All inputs are finite; a program needn't handle non-finite values.
Results may differ from a plain program's by a relative error of at most 0.00007.
Values sent between devices are 32-bit elements; how exact they have to be, the bound alone decides.
A program may use at most 64 MiB of HBM per device.

v0:
```python
import jax
import jax.numpy as jnp
from jax import lax
from jax.sharding import PartitionSpec as P

B = 256
P_SIZE = 32


def passed_along(value, axis, by):
    peers = lax.axis_size(axis)
    pairs = [(i, i + by) for i in range(peers) if 0 <= i + by < peers]
    return lax.ppermute(value, axis, pairs)


def broadcast(block, axis, holder):
    block = jnp.where(lax.axis_index(axis) == holder, block, jnp.zeros_like(block))
    return lax.psum(block, axis)


def contract_rows(left_side, right_side):
    return lax.dot_general(
        left_side,
        right_side,
        (((0,), (0,)), ((), ())),
        precision=lax.Precision.HIGHEST,
        preferred_element_type=jnp.float32,
    )


def body(normals, design, filter_blocks, regular):
    highest = lax.Precision.HIGHEST
    rows_here, cols_here = normals.shape
    obs_here = design.shape[0]
    row_index = lax.axis_index("row")
    col_index = lax.axis_index("col")
    tiles_per_row = lax.axis_size("col") // lax.axis_size("row")
    prior_rows = passed_along(design, "row", 1)
    blocks = design.reshape(obs_here // P_SIZE, P_SIZE, cols_here)
    before = jnp.concatenate([prior_rows[None], blocks[:-1]], axis=0)
    filtered = jnp.einsum("ij,bjc->bic", filter_blocks[0], blocks, precision=highest)
    filtered = filtered + jnp.einsum("ij,bjc->bic", filter_blocks[1], before, precision=highest)
    filtered = filtered.reshape(obs_here, cols_here)
    columns = lax.all_gather(filtered, "row", axis=0, tiled=True)
    pieces = [
        broadcast(columns, "col", row_index * tiles_per_row + offset)
        for offset in range(tiles_per_row)
    ]
    left_side = jnp.concatenate(pieces, axis=1)
    gram_tile = contract_rows(left_side, columns)
    row_pos = row_index * rows_here + jnp.arange(rows_here, dtype=jnp.int32)
    col_pos = col_index * cols_here + jnp.arange(cols_here, dtype=jnp.int32)
    reg_rows = lax.dynamic_slice_in_dim(regular, row_index * rows_here, rows_here)
    system = normals + gram_tile
    system = system + jnp.where(row_pos[:, None] == col_pos[None, :], reg_rows[:, None], 0.0)
    top_strip = broadcast(system[:B], "row", 0)
    corner = broadcast(top_strip[:, :B], "col", 0)
    factor = jnp.linalg.cholesky(corner)
    inverse = jax.scipy.linalg.solve_triangular(factor, jnp.eye(B, dtype=jnp.float32), lower=True)
    col_panel = lax.dot_general(
        top_strip,
        inverse,
        (((0,), (1,)), ((), ())),
        precision=highest,
        preferred_element_type=jnp.float32,
    )
    shares = [
        broadcast(col_panel, "col", row_index * tiles_per_row + offset)
        for offset in range(tiles_per_row)
    ]
    row_panel = jnp.concatenate(shares, axis=0)
    update = lax.dot_general(
        row_panel,
        col_panel,
        (((1,), (1,)), ((), ())),
        precision=highest,
        preferred_element_type=jnp.float32,
    )
    trailing = system - update
    padded = jnp.pad(row_panel, ((0, 0), (0, cols_here - B)))
    return jnp.where(col_pos[None, :] < B, padded, trailing)


def solution(mesh):
    in_specs = (P("row", "col"), P("row", "col"), P(), P())
    out_specs = P("row", "col")
    return jax.shard_map(body, mesh=mesh, in_specs=in_specs, out_specs=out_specs, check_vma=False)
```

profile of v0, /device:TPU:1, one launch (start us, length us, event | category | flops | bytes accessed | tf_op | source)
XLA Modules:
  0.0 1246.8 jit_solution(5678547278901079567)
XLA Ops:
  6.5 0.0 all-reduce.15.cloned.1.call-start
  6.5 9.6 collective-permute-start
  16.2 1.0 fusion.26
  17.2 0.5 collective-permute-done
  17.6 0.9 fusion.11
  18.5 66.3 %all-gather = f32[1,512,384]{2,1,0:T(8,128)S(1)} all-gather(f32[1,32,384]{2,1,0:T(8,128)S(1)} %fusion.11), channel_id=2, replica_groups=mesh['row'=16,'col'=32] {'row'}, dimensions={1}, use_global_device_ids=true | all-gather | bytes 835584 | tf_op jit(solution)/shard_map/all_gather | solution.py:44
  84.8 1.3 bitcast_select_fusion.1
  86.1 0.0 copy-start
  86.1 0.0 all-reduce.15.cloned.1.call-update
  86.1 0.0 all-reduce.9.cloned.1.call-start
  86.2 1.2 copy-done
  87.4 0.4 copy.5
  87.7 0.8 dynamic_slice.3
  88.5 296.6 %all-reduce.15.cloned.1.call-done = (f32[512,384]{1,0:T(8,128)}, f32[512,384]{1,0:T(8,128)}) async-done(((f32[512,384]{1,0:T(8,128)}, f32[512,384]{1,0:T(8,128)}), (f32[512,384]{1,0:T(8,128)}, f32[512,384]{1,0:T(8,128)})) %all-reduce.15.cloned.1.call-update) | async-done | bytes 1572880 | tf_op jit(solution)/shard_map/psum | solution.py:18
  385.1 3.6 fusion.7
  388.7 0.8 slice_select_fusion
  389.5 0.0 all-reduce.9.cloned.1.call-update
  389.5 0.0 all-reduce.11.cloned.1.call-start
  389.5 195.5 %all-reduce.9.cloned.1.call-done = f32[256,384]{0,1:T(8,128)} async-done(((f32[256,384]{0,1:T(8,128)}), f32[256,384]{0,1:T(8,128)}) %all-reduce.9.cloned.1.call-update) | async-done | bytes 393232 | tf_op jit(solution)/shard_map/psum | solution.py:18
  585.0 1.7 slice_select_fusion.1
  586.7 0.0 all-reduce.11.cloned.1.call-update
  586.7 0.2 all-reduce.13.cloned.1.call-start
  587.0 294.3 %all-reduce.11.cloned.1.call-done = f32[256,256]{0,1:T(8,128)} async-done(((f32[256,256]{0,1:T(8,128)}), f32[256,256]{0,1:T(8,128)}) %all-reduce.11.cloned.1.call-update) | async-done | bytes 262160 | tf_op jit(solution)/shard_map/psum | solution.py:18
  881.3 1.1 copy.7
  882.4 1.0 fusion.17
  883.4 11.7 cholesky.49
  895.1 9.8 custom-call.15
  905.0 0.2 fusion.22
  905.2 0.3 convolution_subtract_fusion.2
  905.4 11.7 cholesky.103
  917.2 0.1 copy.10
  917.3 0.1 copy.9
  917.4 0.1 copy.8
  917.5 0.7 compare_reduce_fusion
  919.7 0.1 triangular_solve.63
  919.7 0.0 copy-start.1
  919.7 4.5 while.1
  919.9 0.6 fusion.43
  920.5 1.4 dynamic-slice.7
  922.0 0.1 copy.20
  922.1 0.6 fusion.43
  922.7 1.4 dynamic-slice.7
  924.1 0.1 copy.20
  924.3 19.7 %custom-call.16 = f32[2,128,128]{1,2,0:T(8,128)S(1)} custom-call(f32[2,128,128]{2,1,0:T(8,128)S(1)} %get-tuple-element.12), custom_call_target="InvertDiagBlocksLowerTriangular" | custom-call | tf_op jit(solution)/shard_map/jit(_solve_triangular)/triangular_solve | solution.py:59
  943.9 0.3 fusion.18
  944.2 0.3 convolution_subtract_fusion.1
  944.5 0.3 fusion.21
  944.9 0.0 copy-done.1
  944.9 0.5 fusion.13
  945.4 0.2 copy.12
  945.6 0.9 broadcast_select_fusion
  946.5 0.0 all-reduce.13.cloned.1.call-update
  946.5 289.1 %all-reduce.13.cloned.1.call-done = (f32[384,256]{0,1:T(8,128)}, f32[384,256]{0,1:T(8,128)}) async-done(((f32[384,256]{0,1:T(8,128)}, f32[384,256]{0,1:T(8,128)}), (f32[384,256]{0,1:T(8,128)}, f32[384,256]{0,1:T(8,128)})) %all-reduce.13.cloned.1.call-update) | async-done | bytes 786448 | tf_op jit(solution)/shard_map/psum | solution.py:18
  1235.6 1.0 constant_dynamic-update-slice_fusion.1
  1236.6 1.0 constant_dynamic-update-slice_fusion
  1237.7 1.2 fusion.10
  1238.9 1.4 copy.15
  (17 shorter events, 0.2 us)
Async XLA Ops:
  6.5 378.5 %all-reduce.15.cloned.1.call-start = ((), (), s32[]{:S(2)}) async-start(), calls=%async_computation.3 | async-start | bytes 3145728 | tf_op jit(solution)/shard_map/psum | solution.py:18
  6.5 11.1 collective-permute-start
  86.1 1.3 copy-start
  86.1 498.9 %all-reduce.9.cloned.1.call-start = ((), (), s32[]{:S(2)}) async-start(), calls=%async_computation | async-start | bytes 786432 | tf_op jit(solution)/shard_map/psum | solution.py:18
  389.5 491.8 %all-reduce.11.cloned.1.call-start = ((), (), s32[]{:S(2)}) async-start(), calls=%async_computation.1 | async-start | bytes 524288 | tf_op jit(solution)/shard_map/psum | solution.py:18
  586.7 648.9 %all-reduce.13.cloned.1.call-start = ((), (), s32[]{:S(2)}) async-start(), calls=%async_computation.2 | async-start | bytes 1572864 | tf_op jit(solution)/shard_map/psum | solution.py:18
  919.7 25.1 %copy-start.1 = (f32[256,384]{0,1:T(8,128)S(1)}, f32[256,384]{0,1:T(8,128)}, u32[]{:S(2)}) copy-start(f32[256,384]{0,1:T(8,128)} %all-reduce.9.cloned.1.call-done) | copy-start | bytes 1179652
Sparse Core Ops, SparseCore 0:
  86.2 298.8 all-reduce.14
  389.6 195.3 all-reduce.8
  587.9 293.3 all-reduce.10
  946.6 288.9 all-reduce.12
where the time goes:
time: 1250 us
  waiting for transfers between devices  1080 us (86%)
  blocking collectives  66.3 us (5%)
  other arithmetic  59.4 us (5%)
  between operations  14.7 us (1%)
    psum x4, waiting for transfers between devices, broadcast(): return lax.psum(block, axis)  1080 us
    all_gather x1, blocking collectives, body(): columns = lax.all_gather(filtered, 'row', axis=0, tiled=True)  66.3 us
    another operation x6, other arithmetic, body(): factor = jnp.linalg.cholesky(corner)  34 us
  transfers between devices with their start and end apart: 5, of which 5 were waited for; matrix products, arithmetic and copies ran while one was open for 0% of the time, Pallas kernels for 0%

commit v1 on v0

--- a/solution.py
+++ b/solution.py
@@ -15,7 +15,7 @@
 
 def broadcast(block, axis, holder):
     block = jnp.where(lax.axis_index(axis) == holder, block, jnp.zeros_like(block))
-    return lax.psum(block, axis)
+    return jnp.sum(lax.all_gather(block, axis), axis=0)
 
 
 def contract_rows(left_side, right_side):

time: 1250 us -> 907 us (0.73)
  waiting for transfers between devices: 1080 us -> 706 us
  other arithmetic: 59.4 us -> 92.8 us
    psum x4 -> x0, waiting for transfers between devices: 1080 us -> none  [broadcast(): return lax.psum(block, axis)]
    all_gather x0 -> x6, waiting for transfers between devices: none -> 704 us  [broadcast(): return jnp.sum(lax.all_gather(block, axis), axis=0)]
    reduce_sum x0 -> x6, other arithmetic: none -> 36.1 us  [broadcast(): return jnp.sum(lax.all_gather(block, axis), axis=0)]
  transfers between devices with their start and end apart: 5 -> 7, of which waited for: 5 -> 7; matrix products, arithmetic and copies ran while one was open for 0% -> 2% of each run, Pallas kernels for 0% -> 0%
where the time goes in v1:
time: 907 us; the launch traced here: 906 us
  waiting for transfers between devices  706 us (78%)
  other arithmetic  92.8 us (10%)
  blocking collectives  66.3 us (7%)
  between operations  15 us (2%)
  matrix products  11.4 us (1%)
  starting transfers between devices  10 us (1%)
    all_gather x6, waiting for transfers between devices, broadcast(): return jnp.sum(lax.all_gather(block, axis), axis=0)  704 us
    all_gather x1, blocking collectives, body(): columns = lax.all_gather(filtered, 'row', axis=0, tiled=True)  66.3 us
    reduce_sum x6, other arithmetic, broadcast(): return jnp.sum(lax.all_gather(block, axis), axis=0)  36.1 us
    another operation x6, other arithmetic, body(): factor = jnp.linalg.cholesky(corner)  34 us
    another operation x3, other arithmetic, body(): jax.scipy.linalg.solve_triangular(factor, jnp.eye(B, dtype=jnp.float32),...  19.7 us
  transfers between devices with their start and end apart: 7, of which 7 were waited for; matrix products, arithmetic and copies ran while one was open for 2% of the time, Pallas kernels for 0%

profile of v1, /device:TPU:1, one launch (start us, length us, event | category | flops | bytes accessed | tf_op | source)
XLA Modules:
  0.0 906.2 jit_solution(3790791137745188807)
XLA Ops:
  6.5 0.0 all-gather.16.cloned.1.call-start
  6.5 9.6 %collective-permute-start = (f32[32,384]{1,0:T(8,128)}, f32[32,384]{1,0:T(8,128)S(1)}, u32[]{:S(2)}, u32[]{:S(2)}) collective-permute-start(f32[32,384]{1,0:T(8,128)} %param.5), channel_id=1, source_target_pairs={{0,32},{32,64},{64,96},{96,128},{128,160},{160,192},{192,224},{224... | collective-permute-start | bytes 147464 | tf_op jit(solution)/shard_map/ppermute | solution.py:13
  16.2 1.0 fusion.26
  17.2 0.5 collective-permute-done
  17.6 0.9 fusion.11
  18.5 66.3 %all-gather = f32[1,512,384]{2,1,0:T(8,128)S(1)} all-gather(f32[1,32,384]{2,1,0:T(8,128)S(1)} %fusion.11), channel_id=2, replica_groups=mesh['row'=16,'col'=32] {'row'}, dimensions={1}, use_global_device_ids=true | all-gather | bytes 835584 | tf_op jit(solution)/shard_map/all_gather | solution.py:44
  84.8 1.3 bitcast_select_fusion.1
  86.1 0.0 all-gather.16.cloned.1.call-update
  86.1 0.0 all-gather.14.cloned.1.call-start
  86.2 0.7 all-gather.14.cloned.1.call-update
  86.9 0.0 all-gather.18.cloned.1.call-start
  86.9 0.8 dynamic_slice.3
  87.7 152.2 %all-gather.16.cloned.1.call-done = f32[16384,384]{1,0:T(8,128)} async-done(((f32[512,384]{1,0:T(8,128)}), f32[16384,384]{1,0:T(8,128)}) %all-gather.16.cloned.1.call-update) | async-done | bytes 25165840 | tf_op jit(solution)/shard_map/all_gather | solution.py:18
  239.9 9.1 %reduce_sum.55 = f32[512,384]{1,0:T(8,128)S(1)} reduce(f32[32,512,384]{2,1,0:T(8,128)} %bitcast.57, f32[]{:T(128)} %constant.100.clone.1), dimensions={0}, to_apply=%region_1.2 | reduce | flops 6094848 | bytes 25952260 | tf_op jit(solution)/shard_map/reduce_sum | solution.py:18
  249.1 140.9 %all-gather.14.cloned.1.call-done = f32[16384,384]{1,0:T(8,128)} async-done(((f32[512,384]{1,0:T(8,128)}), f32[16384,384]{1,0:T(8,128)}) %all-gather.14.cloned.1.call-update) | async-done | bytes 25165840 | tf_op jit(solution)/shard_map/all_gather | solution.py:18
  390.0 9.1 %reduce_sum.54 = f32[512,384]{1,0:T(8,128)S(1)} reduce(f32[32,512,384]{2,1,0:T(8,128)} %bitcast.58, f32[]{:T(128)} %constant.100.clone.1), dimensions={0}, to_apply=%region_0.1 | reduce | flops 6094848 | bytes 25952260 | tf_op jit(solution)/shard_map/reduce_sum | solution.py:18
  399.1 4.0 fusion.7
  403.2 0.8 slice_select_fusion
  403.9 0.0 all-gather.18.cloned.1.call-update
  404.0 0.0 all-gather.20.cloned.1.call-start
  404.0 176.2 %all-gather.18.cloned.1.call-done = f32[4096,384]{1,0:T(8,128)} async-done(((f32[256,384]{1,0:T(8,128)}), f32[4096,384]{1,0:T(8,128)}) %all-gather.18.cloned.1.call-update) | async-done | bytes 6291472 | tf_op jit(solution)/shard_map/all_gather | solution.py:18
  580.2 3.1 reduce_sum.56
  583.3 0.7 slice_select_fusion.1
  584.1 0.0 all-gather.20.cloned.1.call-update
  584.1 0.2 all-gather.24.cloned.1.call-start
  584.4 70.0 %all-gather.20.cloned.1.call-done = f32[8192,256]{1,0:T(8,128)} async-done(((f32[256,256]{1,0:T(8,128)}), f32[8192,256]{1,0:T(8,128)}) %all-gather.20.cloned.1.call-update) | async-done | bytes 8388624 | tf_op jit(solution)/shard_map/all_gather | solution.py:18
  654.4 3.9 reduce_sum.57
  658.3 0.1 copy.6
  658.5 11.7 %cholesky.49 = f32[128,128]{1,0:T(8,128)S(1)} custom-call(f32[128,128]{1,0:T(8,128)S(1)} %cholesky.115), custom_call_target="Cholesky" | custom-call | tf_op jit(solution)/shard_map/jit(cholesky)/cholesky | solution.py:58
  670.3 9.8 %custom-call.15 = f32[1,128,128]{1,2,0:T(8,128)S(1)} custom-call(f32[1,128,128]{2,1,0:T(8,128)S(1)} %get-tuple-element.30), custom_call_target="InvertDiagBlocksLowerTriangular" | custom-call | tf_op jit(solution)/shard_map/jit(cholesky)/cholesky | solution.py:58
  680.1 0.2 constant_dynamic-update-slice_fusion.1
  680.3 0.3 convolution_subtract_fusion.2
  680.6 11.7 %cholesky.103 = f32[128,128]{1,0:T(8,128)S(1)} custom-call(f32[128,128]{1,0:T(8,128)S(1)} %convolution_subtract_fusion.2), custom_call_target="Cholesky" | custom-call | tf_op jit(solution)/shard_map/jit(cholesky)/cholesky | solution.py:58
  692.3 0.7 compare_reduce_fusion
  694.4 0.1 triangular_solve.63
  694.5 4.3 while.1
  694.7 0.6 fusion.43
  695.3 1.4 bitcast_dynamic-update-slice_fusion.2
  696.7 0.6 fusion.43
  697.3 1.4 bitcast_dynamic-update-slice_fusion.2
  698.8 19.7 %custom-call.16 = f32[2,128,128]{1,2,0:T(8,128)S(1)} custom-call(f32[2,128,128]{2,1,0:T(8,128)S(1)} %get-tuple-element.12), custom_call_target="InvertDiagBlocksLowerTriangular" | custom-call | tf_op jit(solution)/shard_map/jit(_solve_triangular)/triangular_solve | solution.py:59
  718.5 0.3 fusion.18
  718.7 0.3 convolution_subtract_fusion.1
  719.0 0.3 fusion.21
  719.3 1.7 broadcast_select_fusion.1
  721.1 0.0 all-gather.24.cloned.1.call-update
  721.1 0.0 all-gather.22.cloned.1.call-start
  721.1 0.5 all-gather.22.cloned.1.call-update
  721.7 83.2 %all-gather.24.cloned.1.call-done = f32[12288,256]{1,0:T(8,128)} async-done(((f32[384,256]{1,0:T(8,128)}), f32[12288,256]{1,0:T(8,128)}) %all-gather.24.cloned.1.call-update) | async-done | bytes 12582928 | tf_op jit(solution)/shard_map/all_gather | solution.py:18
  804.9 5.4 reduce_sum.59
  810.3 81.2 %all-gather.22.cloned.1.call-done = f32[12288,256]{1,0:T(8,128)} async-done(((f32[384,256]{1,0:T(8,128)}), f32[12288,256]{1,0:T(8,128)}) %all-gather.22.cloned.1.call-update) | async-done | bytes 12582928 | tf_op jit(solution)/shard_map/all_gather | solution.py:18
  891.5 5.4 reduce_sum.58
  896.9 0.1 pad_maximum_fusion
  897.0 2.4 fusion.10
  (14 shorter events, 0.2 us)
Async XLA Ops:
  6.5 233.4 %all-gather.16.cloned.1.call-start = ((), (), s32[]{:S(2)}) async-start(), calls=%async_computation.1 | async-start | bytes 25952256 | tf_op jit(solution)/shard_map/all_gather | solution.py:18
  6.5 11.1 %collective-permute-start = (f32[32,384]{1,0:T(8,128)}, f32[32,384]{1,0:T(8,128)S(1)}, u32[]{:S(2)}, u32[]{:S(2)}) collective-permute-start(f32[32,384]{1,0:T(8,128)} %param.5), channel_id=1, source_target_pairs={{0,32},{32,64},{64,96},{96,128},{128,160},{160,192},{192,224},{224... | collective-permute-start | bytes 147464 | tf_op jit(solution)/shard_map/ppermute | solution.py:13
  86.1 303.9 %all-gather.14.cloned.1.call-start = ((), (), s32[]{:S(2)}) async-start(), calls=%async_computation | async-start | bytes 25952256 | tf_op jit(solution)/shard_map/all_gather | solution.py:18
  86.9 493.4 %all-gather.18.cloned.1.call-start = ((), (), s32[]{:S(2)}) async-start(), calls=%async_computation.2 | async-start | bytes 6684672 | tf_op jit(solution)/shard_map/all_gather | solution.py:18
  404.0 250.4 %all-gather.20.cloned.1.call-start = ((), (), s32[]{:S(2)}) async-start(), calls=%async_computation.3 | async-start | bytes 8650752 | tf_op jit(solution)/shard_map/all_gather | solution.py:18
  584.1 220.8 %all-gather.24.cloned.1.call-start = ((), (), s32[]{:S(2)}) async-start(), calls=%async_computation.5 | async-start | bytes 12976128 | tf_op jit(solution)/shard_map/all_gather | solution.py:18
  721.1 170.4 %all-gather.22.cloned.1.call-start = ((), (), s32[]{:S(2)}) async-start(), calls=%async_computation.4 | async-start | bytes 12976128 | tf_op jit(solution)/shard_map/all_gather | solution.py:18
Sparse Core Ops, SparseCore 0:
  86.2 153.6 all-gather.15
  242.1 147.8 all-gather.13
  404.1 176.0 all-gather.17
  584.2 70.1 all-gather.19
  721.2 83.6 all-gather.23
  806.9 84.5 all-gather.21
